TPU v7x, 32 devices: a whole 2x2x4 slice. The times are simulated.
32 devices in a mesh: island: 4 (over y, core), section: 4 (over z), tensor: 2 (over x).
Axes of the slice: x: 2, y: 2, z: 4, core: 2. Of those that a mesh axis runs over, the one named last changes fastest.
Arguments:
- hidden: bfloat16 [4, 4, 256, 8192], P('island', 'section', 'tensor'), may hold values from -6 to 6
- norm_gain: bfloat16 [4, 8192], P('section'), may hold values from 0.099609375 to 1.8984375
- grad_above: bfloat16 [4, 256, 8192], P('island', 'tensor'), may hold values from -6 to 6
- key_cot: bfloat16 [4, 4, 256, 1024], P('island', 'section', None, 'tensor'), may hold values from -6 to 6
- value_cot: bfloat16 [4, 4, 256, 1024], P('island', 'section', None, 'tensor'), may hold values from -6 to 6
- local_key: bfloat16 [4, 4, 8192, 1024], P('island', 'section', None, 'tensor'), may hold values from -6 to 6
- local_value: bfloat16 [4, 4, 8192, 1024], P('island', 'section', None, 'tensor'), may hold values from -6 to 6
- anchor_key: float32 [4, 8192, 1024], P('section', 'island', 'tensor'), may hold values from -6 to 6
- anchor_value: float32 [4, 8192, 1024], P('section', 'island', 'tensor'), may hold values from -6 to 6
- momentum_key: float32 [4, 8192, 1024], P('section', 'island', 'tensor'), may hold values from -4 to 4
- momentum_value: float32 [4, 8192, 1024], P('section', 'island', 'tensor'), may hold values from -4 to 4
Outputs:
- anchor_key_new: float32 [4, 8192, 1024], P('section', 'island', 'tensor')
- anchor_value_new: float32 [4, 8192, 1024], P('section', 'island', 'tensor')
- momentum_key_new: float32 [4, 8192, 1024], P('section', 'island', 'tensor')
- momentum_value_new: float32 [4, 8192, 1024], P('section', 'island', 'tensor')
- input_grad: bfloat16 [4, 4, 256, 8192], P('island', 'section', 'tensor')
All inputs are finite; a program needn't handle non-finite values.
Results may differ from a plain program's by a relative error of at most 0.024.
Values may be sent and summed in bfloat16 or wider, within the bound.
No kernel may reach another device: no remote copies, remote signals or barrier semaphores. Data moves between devices by JAX's collectives and lax.ppermute only.
A program may use at most 128 MiB of HBM per device.

v0:
```python
import jax
import jax.numpy as jnp
from jax import lax
from jax.sharding import PartitionSpec as P

epsilon = 1e-05
inner_rate = 0.5
outer_rate = 0.7
outer_beta = 0.9


def from_behind(block, axis, distance):
    devices = range(lax.axis_size(axis))
    route = [(i - distance, i) for i in devices if i - distance in devices]
    return lax.ppermute(block, axis, route)


def contract_rows(left, right):
    return lax.dot_general(
        left, right, (((0,), (0,)), ((), ())), preferred_element_type=jnp.float32
    )


def contract_cols(left, right):
    return lax.dot_general(
        left, right, (((1,), (1,)), ((), ())), preferred_element_type=jnp.float32
    )


def outer_update(anchor, momentum, mean_delta):
    momentum_new = outer_beta * momentum + mean_delta
    return (anchor - outer_rate * (mean_delta + outer_beta * momentum_new), momentum_new)


def local(
    hidden,
    norm_gain,
    grad_above,
    key_cot,
    value_cot,
    local_key,
    local_value,
    anchor_key,
    anchor_value,
    momentum_key,
    momentum_value,
):
    resid = hidden[0, 0].astype(jnp.float32)
    gains = norm_gain[0].astype(jnp.float32)
    features = resid.shape[1]
    factor = float(features) ** (-0.5)
    inverse_rms = lax.rsqrt(jnp.mean(resid * resid, axis=-1, keepdims=True) + epsilon)
    normed = (resid * inverse_rms * gains).astype(jnp.bfloat16)
    key_rows = key_cot[0, 0]
    value_rows = value_cot[0, 0]
    weight_key = local_key[0, 0]
    weight_value = local_value[0, 0]
    piece = lax.all_gather(normed, "tensor", axis=0, tiled=True)
    key_piece = key_rows
    value_piece = value_rows
    grad_key = contract_rows(piece, key_piece)
    grad_value = contract_rows(piece, value_piece)
    new_key = weight_key.astype(jnp.float32) - inner_rate * (grad_key * factor)
    new_value = weight_value.astype(jnp.float32) - inner_rate * (grad_value * factor)
    key_piece = key_rows
    value_piece = value_rows
    upstream = lax.psum_scatter(
        (
            (contract_cols(key_piece, weight_key) + contract_cols(value_piece, weight_value))
            * factor
        ).astype(jnp.bfloat16),
        "tensor",
        scatter_dimension=0,
        tiled=True,
    ).astype(jnp.float32)
    scaled = gains * upstream
    branch = inverse_rms * scaled - resid * inverse_rms**3 * jnp.mean(
        resid * scaled, axis=-1, keepdims=True
    )
    is_top = (lax.axis_index("section") == lax.axis_size("section") - 1).astype(jnp.float32)
    own_term = branch + is_top * grad_above[0].astype(jnp.float32)
    running = own_term
    for turn in range(lax.axis_size("section") - 1):
        running = own_term + from_behind(running.astype(jnp.bfloat16), "section", -1).astype(
            running.dtype
        )
    input_grad = running.astype(jnp.bfloat16)[None, None]
    islands = lax.axis_size("island")
    summed_key, summed_value = (
        lax.psum_scatter(
            new_key.astype(jnp.bfloat16), "island", scatter_dimension=0, tiled=True
        ).astype(jnp.float32),
        lax.psum_scatter(
            new_value.astype(jnp.bfloat16), "island", scatter_dimension=0, tiled=True
        ).astype(jnp.float32),
    )
    mean_key = anchor_key[0] - summed_key / islands
    mean_value = anchor_value[0] - summed_value / islands
    anchor_key_new, momentum_key_new = outer_update(anchor_key[0], momentum_key[0], mean_key)
    anchor_value_new, momentum_value_new = outer_update(
        anchor_value[0], momentum_value[0], mean_value
    )
    return (
        anchor_key_new[None],
        anchor_value_new[None],
        momentum_key_new[None],
        momentum_value_new[None],
        input_grad,
    )


def solution(mesh):
    placed = (
        P("island", "section", "tensor", None),
        P("section", None),
        P("island", "tensor", None),
        P("island", "section", None, "tensor"),
        P("island", "section", None, "tensor"),
        P("island", "section", None, "tensor"),
        P("island", "section", None, "tensor"),
        P("section", "island", "tensor"),
        P("section", "island", "tensor"),
        P("section", "island", "tensor"),
        P("section", "island", "tensor"),
    )
    return jax.shard_map(
        local,
        mesh=mesh,
        in_specs=placed,
        out_specs=(
            P("section", "island", "tensor"),
            P("section", "island", "tensor"),
            P("section", "island", "tensor"),
            P("section", "island", "tensor"),
            P("island", "section", "tensor", None),
        ),
        check_vma=False,
    )
```

profile of v0, /device:TPU:0, one launch (start us, length us, event | category | flops | bytes accessed | tf_op | source)
XLA Modules:
  0.0 336.5 jit_solution(11189967100800048256)
XLA Ops:
  7.2 0.0 copy-start
  7.2 0.0 reduce-scatter.8.cloned.1.call-start
  7.2 0.9 copy-done
  8.1 5.8 %fusion.3 = f32[256,8192]{1,0:T(8,128)S(1)} fusion(bf16[1,1,8192,512]{3,2,1,0:T(8,128)(2,1)} %param.16, bf16[1,1,256,512]{3,2,1,0:T(8,128)(2,1)S(1)} %copy-done), kind=kOutput, calls=%fused_computation.6 | convolution fusion | flops 2147483648 | bytes 17039360 | tf_op jit(solution)/shard_map/dot_general | solution.py:25
  13.9 7.9 %fusion.1 = bf16[256,8192]{1,0:T(8,128)(2,1)} fusion(f32[256,8192]{1,0:T(8,128)S(1)} %fusion.3, bf16[1,1,8192,512]{3,2,1,0:T(8,128)(2,1)} %param.17, bf16[1,1,256,512]{3,2,1,0:T(8,128)(2,1)S(1)} %copy-done.7), kind=kOutput, calls=%fused_computation.4 | convolution fusion | flops 2153775104 | bytes 21233664 | tf_op jit(solution)/shard_map/dot_general | solution.py:25
  21.8 0.0 reduce-scatter.8.cloned.1.call-update
  21.8 0.0 all-gather.2.cloned.1.call-start
  21.9 0.7 copy-done.8
  22.6 56.5 %reduce-scatter.8.cloned.1.call-done = bf16[128,8192]{1,0:T(8,128)(2,1)} async-done(((bf16[256,8192]{1,0:T(8,128)(2,1)}), bf16[128,8192]{1,0:T(8,128)(2,1)}) %reduce-scatter.8.cloned.1.call-update) | async-done | bytes 2097168 | tf_op jit(solution)/shard_map/reduce_scatter | solution.py:67
  79.1 2.8 fusion.11
  81.9 0.0 copy-done.5
  81.9 4.3 %fusion.21 = (bf16[128,8192]{1,0:T(8,128)(2,1)}, f32[128,8192]{1,0:T(8,128)}, bf16[128,8192]{1,0:T(8,128)(2,1)}) fusion(bf16[1,128,8192]{2,1,0:T(8,128)(2,1)S(1)} %copy-done.5, f32[]{:T(128)S(6)} %convert_element_type.74, f32[128]{0:T(128)S(1)} %get-tuple-element.16, f32[128]{0:T(128)S(1)} %get-tuple-element.14, bf16[1,1,128,8192]{3,2,1,0:T(8,128)(2,1)S(1)} %copy-done.3, ...), kind=kLoop, calls=%fused_computation.41 | loop fusion | flops 14680064 | bytes 14714372 | tf_op jit(solution)/shard_map/convert_element_type | solution.py:84
  86.3 0.0 all-gather.2.cloned.1.call-update
  86.3 0.0 reduce-scatter.4.cloned.1.call-start
  86.3 56.8 %all-gather.2.cloned.1.call-done = bf16[256,8192]{1,0:T(8,128)(2,1)} async-done(((bf16[128,8192]{1,0:T(8,128)(2,1)}), bf16[256,8192]{1,0:T(8,128)(2,1)}) %all-gather.2.cloned.1.call-update) | async-done | bytes 4194320 | tf_op jit(solution)/shard_map/all_gather | solution.py:58
  143.2 8.2 %subtract_convert_fusion.1 = bf16[8192,512]{1,0:T(8,128)(2,1)} fusion(bf16[256,8192]{1,0:T(8,128)(2,1)} %all-gather.2.cloned.1.call-done, bf16[1,1,8192,512]{3,2,1,0:T(8,128)(2,1)} %param.16, bf16[1,1,256,512]{3,2,1,0:T(8,128)(2,1)S(1)} %copy-done), kind=kOutput, calls=%fused_computation.1 | convolution fusion | flops 2164260864 | bytes 21233664 | tf_op jit(solution)/shard_map/dot_general | solution.py:19
  151.3 0.0 reduce-scatter.4.cloned.1.call-update
  151.4 0.0 reduce-scatter.6.cloned.1.call-start
  151.4 8.7 %subtract_convert_fusion = bf16[8192,512]{1,0:T(8,128)(2,1)} fusion(bf16[256,8192]{1,0:T(8,128)(2,1)} %all-gather.2.cloned.1.call-done, bf16[1,1,8192,512]{3,2,1,0:T(8,128)(2,1)} %param.17, bf16[1,1,256,512]{3,2,1,0:T(8,128)(2,1)S(1)} %copy-done.7), kind=kOutput, calls=%fused_computation | convolution fusion | flops 2164260864 | bytes 21233664 | tf_op jit(solution)/shard_map/dot_general | solution.py:19
  160.1 0.0 reduce-scatter.6.cloned.1.call-update
  160.1 2.1 copy-done.6
  162.3 1.3 collective-permute-start
  163.6 47.8 %collective-permute-done = bf16[128,8192]{1,0:T(8,128)(2,1)S(1)} collective-permute-done((bf16[128,8192]{1,0:T(8,128)(2,1)S(1)}, bf16[128,8192]{1,0:T(8,128)(2,1)S(1)}, u32[]{:S(2)}, u32[]{:S(2)}) %collective-permute-start) | collective-permute-done | bytes 2097184 | tf_op jit(solution)/shard_map/ppermute | solution.py:15
  211.3 2.9 add_convert_fusion.2
  214.2 1.3 collective-permute-start.1
  215.5 47.1 %collective-permute-done.1 = bf16[128,8192]{1,0:T(8,128)(2,1)S(1)} collective-permute-done((bf16[128,8192]{1,0:T(8,128)(2,1)S(1)}, bf16[128,8192]{1,0:T(8,128)(2,1)S(1)}, u32[]{:S(2)}, u32[]{:S(2)}) %collective-permute-start.1) | collective-permute-done | bytes 2097184 | tf_op jit(solution)/shard_map/ppermute | solution.py:15
  262.6 0.4 add_convert_fusion.1
  263.0 1.5 collective-permute-start.2
  264.5 46.1 %collective-permute-done.2 = bf16[128,8192]{1,0:T(8,128)(2,1)S(1)} collective-permute-done((bf16[128,8192]{1,0:T(8,128)(2,1)S(1)}, bf16[128,8192]{1,0:T(8,128)(2,1)S(1)}, u32[]{:S(2)}, u32[]{:S(2)}) %collective-permute-start.2) | collective-permute-done | bytes 2097184 | tf_op jit(solution)/shard_map/ppermute | solution.py:15
  310.6 1.8 fusion.16
  312.4 8.7 %fusion.14 = (f32[1,2048,512]{2,1,0:T(8,128)}, f32[1,2048,512]{2,1,0:T(8,128)}) fusion(bf16[2048,512]{1,0:T(8,128)(2,1)} %reduce-scatter.4.cloned.1.call-done, f32[1,2048,512]{2,1,0:T(8,128)} %param.18, f32[1,2048,512]{2,1,0:T(8,128)} %param.20), kind=kLoop, calls=%fused_computation.31 | loop fusion | flops 9437184 | bytes 18874368 | tf_op jit(solution)/shard_map/broadcast_in_dim | solution.py:106
  321.2 8.8 %fusion.15 = (f32[1,2048,512]{2,1,0:T(8,128)}, f32[1,2048,512]{2,1,0:T(8,128)}) fusion(bf16[2048,512]{1,0:T(8,128)(2,1)} %reduce-scatter.6.cloned.1.call-done, f32[1,2048,512]{2,1,0:T(8,128)} %param.19, f32[1,2048,512]{2,1,0:T(8,128)} %param.21), kind=kLoop, calls=%fused_computation.32 | loop fusion | flops 9437184 | bytes 18874368 | tf_op jit(solution)/shard_map/broadcast_in_dim | solution.py:107
  (17 shorter events, 0.1 us)
Async XLA Ops:
  7.2 1.0 copy-start
  7.2 6.7 %copy-start.7 = (bf16[1,1,256,512]{3,2,1,0:T(8,128)(2,1)S(1)}, bf16[1,1,256,512]{3,2,1,0:T(8,128)(2,1)}, u32[]{:S(2)}) copy-start(bf16[1,1,256,512]{3,2,1,0:T(8,128)(2,1)} %param.15) | copy-start | bytes 786436
  7.2 71.9 %reduce-scatter.8.cloned.1.call-start = ((), (), s32[]{:S(2)}) async-start(), calls=%async_computation.6 | async-start | bytes 6291456 | tf_op jit(solution)/shard_map/reduce_scatter | solution.py:67
  21.8 0.8 copy-start.8
  21.8 57.3 %copy-start.3 = (bf16[1,1,128,8192]{3,2,1,0:T(8,128)(2,1)S(1)}, bf16[1,1,128,8192]{3,2,1,0:T(8,128)(2,1)}, u32[]{:S(2)}) copy-start(bf16[1,1,128,8192]{3,2,1,0:T(8,128)(2,1)} %param.11) | copy-start | bytes 6291460
  21.8 121.3 %all-gather.2.cloned.1.call-start = ((), (), s32[]{:S(2)}) async-start(), calls=%async_computation.3 | async-start | bytes 6291456 | tf_op jit(solution)/shard_map/all_gather | solution.py:58
  79.1 2.8 copy-start.4
  79.1 2.9 copy-start.5
  86.3 226.1 %reduce-scatter.4.cloned.1.call-start = ((), (), s32[]{:S(2)}) async-start(), calls=%async_computation.4 | async-start | bytes 10485760 | tf_op jit(solution)/shard_map/reduce_scatter | solution.py:90
  151.4 169.8 %reduce-scatter.6.cloned.1.call-start = ((), (), s32[]{:S(2)}) async-start(), calls=%async_computation.5 | async-start | bytes 10485760 | tf_op jit(solution)/shard_map/reduce_scatter | solution.py:93
  160.1 2.2 copy-start.6
  162.3 49.1 %collective-permute-start = (bf16[128,8192]{1,0:T(8,128)(2,1)S(1)}, bf16[128,8192]{1,0:T(8,128)(2,1)S(1)}, u32[]{:S(2)}, u32[]{:S(2)}) collective-permute-start(bf16[128,8192]{1,0:T(8,128)(2,1)S(1)} %copy-done.6), channel_id=1, source_target_pairs={{2,0},{4,2},{6,4},{3,1},{5,3},{7,5},{10,8},{12,10},{14,12},{11,9},... | collective-permute-start | bytes 6291464 | tf_op jit(solution)/shard_map/ppermute | solution.py:15
  211.3 51.2 %copy-start.2 = (f32[128,8192]{1,0:T(8,128)S(1)}, f32[128,8192]{1,0:T(8,128)}, u32[]{:S(2)}) copy-start(f32[128,8192]{1,0:T(8,128)} %get-tuple-element.8) | copy-start | bytes 12582916
  214.2 48.4 %collective-permute-start.1 = (bf16[128,8192]{1,0:T(8,128)(2,1)S(1)}, bf16[128,8192]{1,0:T(8,128)(2,1)S(1)}, u32[]{:S(2)}, u32[]{:S(2)}) collective-permute-start(bf16[128,8192]{1,0:T(8,128)(2,1)S(1)} %add_convert_fusion.2), channel_id=1, source_target_pairs={{2,0},{4,2},{6,4},{3,1},{5,3},{7,5},{10,8},{12,10},{14,12},{11,9},... | collective-permute-start | bytes 6291464 | tf_op jit(solution)/shard_map/ppermute | solution.py:15
  263.0 47.6 %collective-permute-start.2 = (bf16[128,8192]{1,0:T(8,128)(2,1)S(1)}, bf16[128,8192]{1,0:T(8,128)(2,1)S(1)}, u32[]{:S(2)}, u32[]{:S(2)}) collective-permute-start(bf16[128,8192]{1,0:T(8,128)(2,1)S(1)} %add_convert_fusion.1), channel_id=1, source_target_pairs={{2,0},{4,2},{6,4},{3,1},{5,3},{7,5},{10,8},{12,10},{14,12},{11,9},... | collective-permute-start | bytes 6291464 | tf_op jit(solution)/shard_map/ppermute | solution.py:15
  321.2 8.8 %copy-start.1 = (bf16[1,1,256,512]{3,2,1,0:T(8,128)(2,1)S(1)}, bf16[1,1,256,512]{3,2,1,0:T(8,128)(2,1)}, u32[]{:S(2)}) copy-start(bf16[1,1,256,512]{3,2,1,0:T(8,128)(2,1)} %param.14) | copy-start | bytes 786436
Sparse Core Ops, SparseCore 0:
  21.9 57.0 reduce-scatter.7
  86.4 56.7 all-gather.1
  151.5 71.3 reduce-scatter.3
  225.3 71.3 reduce-scatter.5
where the time goes:
time: 337 us; the launch traced here: 336 us
  waiting for transfers between devices  254 us (75%)
  matrix products  30.5 us (9%)
  other arithmetic  29.8 us (9%)
  between operations  13.9 us (4%)
  starting transfers between devices  4.21 us (1%)
  local copies, waits for them, and re-layouts  3.77 us (1%)
    ppermute x3, waiting for transfers between devices, from_behind(): return lax.ppermute(block, axis, route)  141 us
    all_gather x1, waiting for transfers between devices, local(): piece = lax.all_gather(normed, 'tensor', axis=0, tiled=True)  56.8 us
    reduce_scatter x1, waiting for transfers between devices, local(): lax.psum_scatter(((contract_cols(key_piece, weight_key) + contract_cols(v...  56.5 us
    dot_general x2, matrix products, contract_rows(): lax.dot_general(left, right, (((0,), (0,)), ((), ())), preferred_element_...  16.9 us
    dot_general x2, matrix products, contract_cols(): lax.dot_general(left, right, (((1,), (1,)), ((), ())), preferred_element_...  13.7 us
    broadcast_in_dim x1, other arithmetic, local(): momentum_value_new[None]  8.78 us
    broadcast_in_dim x1, other arithmetic, local(): momentum_key_new[None]  8.75 us
    convert_element_type x3, other arithmetic, local(): running.astype(jnp.bfloat16)  7.59 us
  transfers between devices with their start and end apart: 7, of which 5 were waited for; matrix products, arithmetic and copies ran while one was open for 7% of the time, Pallas kernels for 0%

commit v1 on v0

--- a/solution.py
+++ b/solution.py
@@ -7,6 +7,18 @@
 inner_rate = 0.5
 outer_rate = 0.7
 outer_beta = 0.9
+
+
+def doubled_up(shard, axis, dim):
+    ways, here = (lax.axis_size(axis), lax.axis_index(axis))
+    grown, reach = (shard, 1)
+    while reach < ways:
+        theirs = lax.ppermute(grown, axis, [(d, d ^ reach) for d in range(ways)])
+        mine_first = jnp.concatenate([grown, theirs], axis=dim)
+        theirs_first = jnp.concatenate([theirs, grown], axis=dim)
+        grown = jnp.where(here & reach == 0, mine_first, theirs_first)
+        reach = 2 * reach
+    return grown
 
 
 def from_behind(block, axis, distance):
@@ -55,7 +67,7 @@
     value_rows = value_cot[0, 0]
     weight_key = local_key[0, 0]
     weight_value = local_value[0, 0]
-    piece = lax.all_gather(normed, "tensor", axis=0, tiled=True)
+    piece = doubled_up(normed, "tensor", 0)
     key_piece = key_rows
     value_piece = value_rows
     grad_key = contract_rows(piece, key_piece)

time: 337 us -> 323 us (0.958)
  waiting for transfers between devices: 254 us -> 240 us
    all_gather x1 -> x0, waiting for transfers between devices: 56.8 us -> none  [local(): piece = lax.all_gather(normed, 'tensor', axis=0, tiled=True)]
    ppermute x0 -> x1, waiting for transfers between devices: none -> 47.1 us  [doubled_up(): theirs = lax.ppermute(grown, axis, [(d, d ^ reach) for d in range(ways)])]
    ppermute x3, waiting for transfers between devices: 141 us -> 137 us  [from_behind(): return lax.ppermute(block, axis, route)]
where the time goes in v1:
time: 323 us
  waiting for transfers between devices  240 us (74%)
  matrix products  30.7 us (10%)
  other arithmetic  29.8 us (9%)
  between operations  13.8 us (4%)
  starting transfers between devices  4.53 us (1%)
  local copies, waits for them, and re-layouts  3.75 us (1%)
    ppermute x3, waiting for transfers between devices, from_behind(): return lax.ppermute(block, axis, route)  137 us
    reduce_scatter x1, waiting for transfers between devices, local(): lax.psum_scatter(((contract_cols(key_piece, weight_key) + contract_cols(v...  56.5 us
    ppermute x1, waiting for transfers between devices, doubled_up(): theirs = lax.ppermute(grown, axis, [(d, d ^ reach) for d in range(ways)])  47.1 us
    dot_general x2, matrix products, contract_rows(): lax.dot_general(left, right, (((0,), (0,)), ((), ())), preferred_element_...  17 us
    dot_general x2, matrix products, contract_cols(): lax.dot_general(left, right, (((1,), (1,)), ((), ())), preferred_element_...  13.7 us
    broadcast_in_dim x1, other arithmetic, local(): momentum_value_new[None]  8.78 us
    broadcast_in_dim x1, other arithmetic, local(): momentum_key_new[None]  8.75 us
    convert_element_type x3, other arithmetic, local(): running.astype(jnp.bfloat16)  7.59 us
  transfers between devices with their start and end apart: 7, of which 5 were waited for; matrix products, arithmetic and copies ran while one was open for 7% of the time, Pallas kernels for 0%

profile of v1, /device:TPU:0, one launch (start us, length us, event | category | flops | bytes accessed | tf_op | source)
XLA Modules:
  0.0 322.9 jit_solution(1766624857557282295)
XLA Ops:
  7.2 0.0 copy-start
  7.2 0.0 copy-start.7
  7.2 0.0 reduce-scatter.8.cloned.1.call-start
  7.2 0.9 copy-done
  8.1 5.8 %fusion.3 = f32[256,8192]{1,0:T(8,128)S(1)} fusion(bf16[1,1,8192,512]{3,2,1,0:T(8,128)(2,1)} %param.16, bf16[1,1,256,512]{3,2,1,0:T(8,128)(2,1)S(1)} %copy-done), kind=kOutput, calls=%fused_computation.6 | convolution fusion | flops 2147483648 | bytes 17039360 | tf_op jit(solution)/shard_map/dot_general | solution.py:37
  13.9 7.9 %fusion.1 = bf16[256,8192]{1,0:T(8,128)(2,1)} fusion(f32[256,8192]{1,0:T(8,128)S(1)} %fusion.3, bf16[1,1,8192,512]{3,2,1,0:T(8,128)(2,1)} %param.17, bf16[1,1,256,512]{3,2,1,0:T(8,128)(2,1)S(1)} %copy-done.7), kind=kOutput, calls=%fused_computation.4 | convolution fusion | flops 2153775104 | bytes 21233664 | tf_op jit(solution)/shard_map/dot_general | solution.py:37
  21.8 0.0 reduce-scatter.8.cloned.1.call-update
  21.8 0.0 reduce-scatter.4.cloned.1.call-start
  21.9 0.7 copy-done.8
  22.6 56.5 %reduce-scatter.8.cloned.1.call-done = bf16[128,8192]{1,0:T(8,128)(2,1)} async-done(((bf16[256,8192]{1,0:T(8,128)(2,1)}), bf16[128,8192]{1,0:T(8,128)(2,1)}) %reduce-scatter.8.cloned.1.call-update) | async-done | bytes 2097168 | tf_op jit(solution)/shard_map/reduce_scatter | solution.py:79
  79.1 2.8 fusion.11
  81.9 0.0 copy-done.5
  81.9 4.3 %fusion.23 = (bf16[128,8192]{1,0:T(8,128)(2,1)}, f32[128,8192]{1,0:T(8,128)}, bf16[128,8192]{1,0:T(8,128)(2,1)}) fusion(bf16[1,128,8192]{2,1,0:T(8,128)(2,1)S(1)} %copy-done.5, f32[]{:T(128)S(6)} %convert_element_type.74, f32[128]{0:T(128)S(1)} %get-tuple-element.16, f32[128]{0:T(128)S(1)} %get-tuple-element.14, bf16[1,1,128,8192]{3,2,1,0:T(8,128)(2,1)S(1)} %copy-done.3, ...), kind=kLoop, calls=%fused_computation.44 | loop fusion | flops 14680064 | bytes 14714372 | tf_op jit(solution)/shard_map/convert_element_type | solution.py:96
  86.2 0.4 collective-permute-start
  86.6 47.1 %collective-permute-done = bf16[128,8192]{1,0:T(8,128)(2,1)S(1)} collective-permute-done((bf16[128,8192]{1,0:T(8,128)(2,1)}, bf16[128,8192]{1,0:T(8,128)(2,1)S(1)}, u32[]{:S(2)}, u32[]{:S(2)}) %collective-permute-start) | collective-permute-done | bytes 2097184 | tf_op jit(solution)/shard_map/ppermute | solution.py:16
  133.7 8.3 %subtract_convert_fusion.1 = bf16[8192,512]{1,0:T(8,128)(2,1)} fusion(bf16[1,1,8192,512]{3,2,1,0:T(8,128)(2,1)} %param.16, bf16[128,8192]{1,0:T(8,128)(2,1)S(1)} %collective-permute-done, bf16[128,8192]{1,0:T(8,128)(2,1)} %get-tuple-element.13, pred[]{:T(512)S(6)} %eq.6, bf16[1,1,256,512]{3,2,1,0:T(8,128)(2,1)S(1)} %copy-done), kind=kOutput, calls=%fused_computation.1 | convolution fusion | flops 2183135232 | bytes 21233664 | tf_op jit(solution)/shard_map/dot_general | solution.py:31
  142.0 0.0 reduce-scatter.4.cloned.1.call-update
  142.0 0.0 reduce-scatter.6.cloned.1.call-start
  142.1 8.7 %subtract_convert_fusion = bf16[8192,512]{1,0:T(8,128)(2,1)} fusion(bf16[1,1,8192,512]{3,2,1,0:T(8,128)(2,1)} %param.17, bf16[128,8192]{1,0:T(8,128)(2,1)S(1)} %collective-permute-done, bf16[128,8192]{1,0:T(8,128)(2,1)} %get-tuple-element.13, pred[]{:T(512)S(6)} %eq.6, bf16[1,1,256,512]{3,2,1,0:T(8,128)(2,1)S(1)} %copy-done.7), kind=kOutput, calls=%fused_computation | convolution fusion | flops 2183135232 | bytes 21233664 | tf_op jit(solution)/shard_map/dot_general | solution.py:31
  150.8 0.0 reduce-scatter.6.cloned.1.call-update
  150.8 2.1 copy-done.6
  152.9 1.3 collective-permute-start.1
  154.2 46.4 %collective-permute-done.1 = bf16[128,8192]{1,0:T(8,128)(2,1)S(1)} collective-permute-done((bf16[128,8192]{1,0:T(8,128)(2,1)S(1)}, bf16[128,8192]{1,0:T(8,128)(2,1)S(1)}, u32[]{:S(2)}, u32[]{:S(2)}) %collective-permute-start.1) | collective-permute-done | bytes 2097184 | tf_op jit(solution)/shard_map/ppermute | solution.py:27
  200.6 2.9 add_convert_fusion.2
  203.5 1.3 collective-permute-start.2
  204.8 45.6 %collective-permute-done.2 = bf16[128,8192]{1,0:T(8,128)(2,1)S(1)} collective-permute-done((bf16[128,8192]{1,0:T(8,128)(2,1)S(1)}, bf16[128,8192]{1,0:T(8,128)(2,1)S(1)}, u32[]{:S(2)}, u32[]{:S(2)}) %collective-permute-start.2) | collective-permute-done | bytes 2097184 | tf_op jit(solution)/shard_map/ppermute | solution.py:27
  250.5 0.4 add_convert_fusion.1
  250.9 1.5 collective-permute-start.3
  252.3 44.7 %collective-permute-done.3 = bf16[128,8192]{1,0:T(8,128)(2,1)S(1)} collective-permute-done((bf16[128,8192]{1,0:T(8,128)(2,1)S(1)}, bf16[128,8192]{1,0:T(8,128)(2,1)S(1)}, u32[]{:S(2)}, u32[]{:S(2)}) %collective-permute-start.3) | collective-permute-done | bytes 2097184 | tf_op jit(solution)/shard_map/ppermute | solution.py:27
  297.0 1.8 fusion.16
  298.8 8.7 %fusion.14 = (f32[1,2048,512]{2,1,0:T(8,128)}, f32[1,2048,512]{2,1,0:T(8,128)}) fusion(bf16[2048,512]{1,0:T(8,128)(2,1)} %reduce-scatter.4.cloned.1.call-done, f32[1,2048,512]{2,1,0:T(8,128)} %param.18, f32[1,2048,512]{2,1,0:T(8,128)} %param.20), kind=kLoop, calls=%fused_computation.32 | loop fusion | flops 9437184 | bytes 18874368 | tf_op jit(solution)/shard_map/broadcast_in_dim | solution.py:118
  307.6 8.8 %fusion.15 = (f32[1,2048,512]{2,1,0:T(8,128)}, f32[1,2048,512]{2,1,0:T(8,128)}) fusion(bf16[2048,512]{1,0:T(8,128)(2,1)} %reduce-scatter.6.cloned.1.call-done, f32[1,2048,512]{2,1,0:T(8,128)} %param.19, f32[1,2048,512]{2,1,0:T(8,128)} %param.21), kind=kLoop, calls=%fused_computation.33 | loop fusion | flops 9437184 | bytes 18874368 | tf_op jit(solution)/shard_map/broadcast_in_dim | solution.py:119
  (16 shorter events, 0.1 us)
Async XLA Ops:
  7.2 1.0 copy-start
  7.2 6.7 %copy-start.7 = (bf16[1,1,256,512]{3,2,1,0:T(8,128)(2,1)S(1)}, bf16[1,1,256,512]{3,2,1,0:T(8,128)(2,1)}, u32[]{:S(2)}) copy-start(bf16[1,1,256,512]{3,2,1,0:T(8,128)(2,1)} %param.15) | copy-start | bytes 786436
  7.2 71.9 %reduce-scatter.8.cloned.1.call-start = ((), (), s32[]{:S(2)}) async-start(), calls=%async_computation.5 | async-start | bytes 6291456 | tf_op jit(solution)/shard_map/reduce_scatter | solution.py:79
  21.8 0.8 copy-start.8
  21.8 57.3 %copy-start.3 = (bf16[1,1,128,8192]{3,2,1,0:T(8,128)(2,1)S(1)}, bf16[1,1,128,8192]{3,2,1,0:T(8,128)(2,1)}, u32[]{:S(2)}) copy-start(bf16[1,1,128,8192]{3,2,1,0:T(8,128)(2,1)} %param.11) | copy-start | bytes 6291460
  21.8 277.0 %reduce-scatter.4.cloned.1.call-start = ((), (), s32[]{:S(2)}) async-start(), calls=%async_computation.3 | async-start | bytes 10485760 | tf_op jit(solution)/shard_map/reduce_scatter | solution.py:102
  79.1 2.8 copy-start.4
  79.1 2.9 copy-start.5
  86.2 47.4 %collective-permute-start = (bf16[128,8192]{1,0:T(8,128)(2,1)}, bf16[128,8192]{1,0:T(8,128)(2,1)S(1)}, u32[]{:S(2)}, u32[]{:S(2)}) collective-permute-start(bf16[128,8192]{1,0:T(8,128)(2,1)} %get-tuple-element.13), channel_id=1, source_target_pairs={{0,1},{1,0},{2,3},{3,2},{4,5},{5,4},{6,7},{7,6},{8,9},{9,8},{10,11... | collective-permute-start | bytes 6291464 | tf_op jit(solution)/shard_map/ppermute | solution.py:16
  142.0 165.5 %reduce-scatter.6.cloned.1.call-start = ((), (), s32[]{:S(2)}) async-start(), calls=%async_computation.4 | async-start | bytes 10485760 | tf_op jit(solution)/shard_map/reduce_scatter | solution.py:105
  150.8 2.2 copy-start.6
  152.9 47.7 %collective-permute-start.1 = (bf16[128,8192]{1,0:T(8,128)(2,1)S(1)}, bf16[128,8192]{1,0:T(8,128)(2,1)S(1)}, u32[]{:S(2)}, u32[]{:S(2)}) collective-permute-start(bf16[128,8192]{1,0:T(8,128)(2,1)S(1)} %copy-done.6), channel_id=1, source_target_pairs={{2,0},{4,2},{6,4},{3,1},{5,3},{7,5},{10,8},{12,10},{14,12},{11,9},... | collective-permute-start | bytes 6291464 | tf_op jit(solution)/shard_map/ppermute | solution.py:27
  200.6 49.8 %copy-start.2 = (f32[128,8192]{1,0:T(8,128)S(1)}, f32[128,8192]{1,0:T(8,128)}, u32[]{:S(2)}) copy-start(f32[128,8192]{1,0:T(8,128)} %get-tuple-element.8) | copy-start | bytes 12582916
  203.5 46.9 %collective-permute-start.2 = (bf16[128,8192]{1,0:T(8,128)(2,1)S(1)}, bf16[128,8192]{1,0:T(8,128)(2,1)S(1)}, u32[]{:S(2)}, u32[]{:S(2)}) collective-permute-start(bf16[128,8192]{1,0:T(8,128)(2,1)S(1)} %add_convert_fusion.2), channel_id=1, source_target_pairs={{2,0},{4,2},{6,4},{3,1},{5,3},{7,5},{10,8},{12,10},{14,12},{11,9},... | collective-permute-start | bytes 6291464 | tf_op jit(solution)/shard_map/ppermute | solution.py:27
  250.9 46.2 %collective-permute-start.3 = (bf16[128,8192]{1,0:T(8,128)(2,1)S(1)}, bf16[128,8192]{1,0:T(8,128)(2,1)S(1)}, u32[]{:S(2)}, u32[]{:S(2)}) collective-permute-start(bf16[128,8192]{1,0:T(8,128)(2,1)S(1)} %add_convert_fusion.1), channel_id=1, source_target_pairs={{2,0},{4,2},{6,4},{3,1},{5,3},{7,5},{10,8},{12,10},{14,12},{11,9},... | collective-permute-start | bytes 6291464 | tf_op jit(solution)/shard_map/ppermute | solution.py:27
  307.6 8.8 %copy-start.1 = (bf16[1,1,256,512]{3,2,1,0:T(8,128)(2,1)S(1)}, bf16[1,1,256,512]{3,2,1,0:T(8,128)(2,1)}, u32[]{:S(2)}) copy-start(bf16[1,1,256,512]{3,2,1,0:T(8,128)(2,1)} %param.14) | copy-start | bytes 786436
Sparse Core Ops, SparseCore 0:
  21.9 57.0 reduce-scatter.7
  142.2 71.3 reduce-scatter.3
  216.2 71.3 reduce-scatter.5
